TPU v7x, 512 devices: a whole 4x8x8 slice. The times are simulated.
512 devices in a mesh: dp: 64 (over x, z, core), tensor: 8 (over y).
Axes of the slice: x: 4, y: 8, z: 8, core: 2. Of those that a mesh axis runs over, the one named last changes fastest.
Arguments:
- q_new: bfloat16 [8192, 8192], P(('dp', 'tensor')), may hold values from -6 to 6
- k_new: bfloat16 [8192, 1024], P(('dp', 'tensor')), may hold values from -8 to 8
- v_new: bfloat16 [8192, 1024], P(('dp', 'tensor')), may hold values from -6 to 6
- hist_kv: bfloat16 [2048, 128, 2, 1024], P('dp', None, None, 'tensor'), may hold values from -8 to 8
- sources: int32 [64, 64, 1], P('dp'), may hold values from 0 to 63; in each aligned block of 64 rows (0 to 63, 64 to 127, ..., all dimensions but the last counted through in order) at most 2 rows name the same one
- block_ids: int32 [64, 64], P('dp'), may hold values from 0 to 31
- hist_len: int32 [64], P('dp'), may hold values from 1 to 64, 3840 in all
Outputs:
- attended: bfloat16 [8192, 8192], P(('dp', 'tensor'))
Inputs may be any that keep to these rules, and one draw needn't show every extreme that they name: `sources`: in each group's list no owner is named in more than 2 slots, and some owner is named in exactly 2 slots. `hist_len`: some group has all 64 slots live.
All inputs are finite; a program needn't handle non-finite values.
Results may differ from a plain program's by a relative error of at most 0.0032.
Values may be sent and summed in bfloat16 or wider, within the bound.
No kernel may reach another device: no remote copies, remote signals or barrier semaphores. Data moves between devices by JAX's collectives and lax.ppermute only.
A program may use at most 64 MiB of HBM per device.

v0:
```python
import math
import jax
import jax.numpy as jnp
from jax import lax
from jax.sharding import PartitionSpec as P

HQ = 64
KVH = 8
HD = 128


def slot_ranks(src_rows):
    count = src_rows.shape[-1]
    order = jnp.arange(count)
    earlier = order[None, :] < order[:, None]
    same = (src_rows[..., :, None] == src_rows[..., None, :]) & earlier
    return jnp.sum(same.astype(jnp.int32), axis=-1)


def owner_table(src_rows, id_rows, ranks, owners, capacity):
    match_owner = src_rows[..., None, :] == owners[:, None]
    slot_index = jnp.arange(capacity)
    match_rank = ranks[..., None, :] == slot_index[:, None]
    hitting = match_owner[..., :, None, :] & match_rank[..., None, :, :]
    return jnp.sum(jnp.where(hitting, id_rows[..., None, None, :], 0), axis=-1)


def local(q_new, k_new, v_new, hist_kv, sources, block_ids, hist_len):
    parts = lax.axis_size("tensor")
    groups = lax.axis_size("dp")
    tok_local, q_width = q_new.shape
    kv_width = k_new.shape[1]
    q_parts = q_new.reshape(tok_local, parts, q_width // parts)
    k_parts = k_new.reshape(tok_local, parts, kv_width // parts)
    v_parts = v_new.reshape(tok_local, parts, kv_width // parts)
    q_here, key_local_part, v_here = (
        lax.all_to_all(q_parts, "tensor", split_axis=1, concat_axis=0, tiled=True),
        lax.all_to_all(k_parts, "tensor", split_axis=1, concat_axis=0, tiled=True),
        lax.all_to_all(v_parts, "tensor", split_axis=1, concat_axis=0, tiled=True),
    )
    new_count = q_here.shape[0]
    kv_heads = kv_width // parts // HD
    per_kv = HQ // KVH
    query_rows = q_here.reshape(new_count, kv_heads, per_kv, HD)
    src_list = sources.reshape(-1)
    slots = src_list.shape[0]
    capacity = max(2, 2 * slots // groups)
    ranks = slot_ranks(src_list)
    all_src, all_ids = (
        lax.all_gather(sources, "dp", axis=0, tiled=True),
        lax.all_gather(block_ids, "dp", axis=0, tiled=True),
    )
    all_src = all_src.reshape(groups, slots)
    owners = jnp.reshape(lax.axis_index("dp"), (1,))
    send_table = owner_table(all_src, all_ids, slot_ranks(all_src), owners, capacity).reshape(
        groups, capacity
    )
    picked = hist_kv[send_table.reshape(-1)]
    block_len = picked.shape[1]
    width = picked.shape[3]
    picked = picked.reshape(groups, capacity, block_len, 2, width)
    where_from = src_list * capacity + ranks
    arrived = lax.all_to_all(picked, "dp", split_axis=0, concat_axis=0, tiled=True)
    arrived = arrived.reshape(groups * capacity, block_len, 2, width)[where_from]
    hist_keys = arrived[:, :, 0]
    hist_vals = arrived[:, :, 1]
    score_scale = 1.0 / math.sqrt(HD)
    step = math.gcd(slots, 8)
    turns = slots // step
    key_blocks = hist_keys.reshape(turns, step * block_len, kv_heads, HD)
    val_blocks = hist_vals.reshape(turns, step * block_len, kv_heads, HD)
    live = jnp.repeat((jnp.arange(slots) < hist_len[0]).reshape(turns, step), block_len, axis=1)
    causal = jnp.arange(new_count)[:, None] >= jnp.arange(new_count)[None, :]
    fresh_turn_scores = (
        jnp.einsum("fusi,pui->usfp", query_rows, key_local_part, preferred_element_type=jnp.float32)
        * score_scale
    )
    fresh_turn_scores = jnp.where(causal[None, None], fresh_turn_scores, -jnp.inf)

    def score_block(keys, mask):
        scores = (
            jnp.einsum("nhgd,khd->hgnk", query_rows, keys, preferred_element_type=jnp.float32)
            * score_scale
        )
        return jnp.where(mask[None, None, None, :], scores, -jnp.inf)

    def max_step(top, inputs):
        keys, mask = inputs
        return (jnp.maximum(top, jnp.max(score_block(keys, mask), axis=-1)), None)

    top, _ = lax.scan(max_step, jnp.max(fresh_turn_scores, axis=-1), (key_blocks, live))

    def sum_step(carry, inputs):
        total, running_sum = carry
        keys, vals, mask = inputs
        weights = jnp.exp(score_block(keys, mask) - top[..., None])
        total = total + jnp.sum(weights, axis=-1)
        running_sum = running_sum + jnp.einsum(
            "hgnk,khd->nhgd", weights.astype(jnp.bfloat16), vals, preferred_element_type=jnp.float32
        )
        return ((total, running_sum), None)

    new_weights = jnp.exp(fresh_turn_scores - top[..., None])
    start_total = jnp.sum(new_weights, axis=-1)
    start_summed = jnp.einsum(
        "vxyl,lvq->yvxq",
        new_weights.astype(jnp.bfloat16),
        v_here,
        preferred_element_type=jnp.float32,
    )
    (total, running_sum), _ = lax.scan(
        sum_step, (start_total, start_summed), (key_blocks, val_blocks, live)
    )
    result = running_sum / jnp.transpose(total, (2, 0, 1))[..., None]
    result = result.astype(jnp.bfloat16).reshape(new_count, 1, kv_heads * per_kv * HD)
    back = lax.all_to_all(result, "tensor", split_axis=0, concat_axis=1, tiled=True)
    return back.reshape(tok_local, q_width)


def solution(mesh):
    return jax.shard_map(
        local,
        mesh=mesh,
        in_specs=(
            P(("dp", "tensor"), None),
            P(("dp", "tensor"), None),
            P(("dp", "tensor"), None),
            P("dp", None, None, "tensor"),
            P("dp", None, None),
            P("dp", None),
            P("dp"),
        ),
        out_specs=P(("dp", "tensor"), None),
        check_vma=False,
    )
```

profile of v0, /device:TPU:1, one launch (start us, length us, event | category | flops | bytes accessed | tf_op | source)
XLA Modules:
  0.0 414.2 jit_solution(10428861804598068745)
XLA Ops:
  0.0 0.0 copy-start
  0.0 1.5 copy_bitcast_fusion.2
  1.5 7.7 %all-to-all-start = ((bf16[16,8,128]{2,0,1:T(8,128)(2,1)}), bf16[16,8,128]{2,0,1:T(8,128)(2,1)S(1)}, u32[]{:S(2)}, u32[]{:S(2)}) async-start(bf16[16,8,128]{2,0,1:T(8,128)(2,1)} %copy_bitcast_fusion.2), calls=%async_computation | async-start | bytes 65536 | tf_op jit(solution)/shard_map/all_to_all | solution.py:38
  9.2 45.8 %all_gather.6 = s32[64,64,1]{1,2,0:T(1,128)S(1)} all-gather(s32[1,64,1]{1,2,0:T(1,128)} %param.15), channel_id=1, replica_groups=mesh['dp'=64,'tensor'=8] {'dp'}, dimensions={0}, use_global_device_ids=true | all-gather | bytes 16640 | tf_op jit(solution)/shard_map/all_gather | solution.py:50
  54.9 1.7 copy.106
  56.6 0.0 all-to-all-done
  56.6 6.9 %all-to-all-start.1 = ((bf16[16,8,1024]{2,0,1:T(8,128)(2,1)}), bf16[16,8,1024]{2,0,1:T(8,128)(2,1)S(1)}, u32[]{:S(2)}, u32[]{:S(2)}) async-start(bf16[16,8,1024]{2,0,1:T(8,128)(2,1)} %bitcast.179), calls=%async_computation.1 | async-start | bytes 524288 | tf_op jit(solution)/shard_map/all_to_all | solution.py:37
  63.6 1.9 convert_reduce_fusion
  65.4 38.3 %all-gather = s32[64,1,64]{2,1,0:T(1,128)S(1)} all-gather(s32[1,1,64]{2,1,0:T(1,128)} %bitcast.232), channel_id=1, replica_groups=mesh['dp'=64,'tensor'=8] {'dp'}, dimensions={0}, use_global_device_ids=true | all-gather | bytes 16640 | tf_op jit(solution)/shard_map/all_gather | solution.py:51
  103.8 0.1 select_reduce_fusion
  103.9 0.1 copy.76
  104.0 0.1 reshape_reshape.3
  104.2 19.5 %gather_fusion = bf16[128,128,2,128]{3,2,1,0:T(2,128)(2,1)} fusion(bf16[32,128,2,128]{3,2,1,0:T(2,128)(2,1)S(1)} %copy-done, s32[1024]{0:T(1024)S(1)} %pad_clamp_fusion.1), kind=kCustom, calls=%fused_computation | custom fusion | bytes 16777728 | tf_op jit(solution)/shard_map/gather | solution.py:58
  123.6 9.1 %copy.77 = bf16[64,2,128,2,128]{4,2,3,1,0:T(8,128)(2,1)} copy(bf16[64,2,128,2,128]{4,3,2,1,0:T(2,128)(2,1)} %bitcast.211) | data formatting | bytes 16777216 | tf_op jit(solution)/shard_map/reshape | solution.py:61
  132.8 0.0 all-to-all-done.1
  132.8 7.2 %all-to-all-start.2 = ((bf16[64,2,128,2,128]{4,2,3,1,0:T(8,128)(2,1)}), bf16[64,2,128,2,128]{4,2,3,1,0:T(8,128)(2,1)}, u32[]{:S(2)}, u32[]{:S(2)}) async-start(bf16[64,2,128,2,128]{4,2,3,1,0:T(8,128)(2,1)} %copy.77), calls=%async_computation.2 | async-start | bytes 16777216 | tf_op jit(solution)/shard_map/all_to_all | solution.py:63
  140.6 0.0 copy-done.2
  140.6 0.2 convert_reduce_fusion.1
  140.8 0.1 broadcast_bitcast_fusion
  140.9 0.6 copy_bitcast_fusion.1
  141.6 0.2 fusion.40
  141.9 183.8 %all-to-all-done.2 = bf16[64,2,128,2,128]{4,2,3,1,0:T(8,128)(2,1)} async-done(((bf16[64,2,128,2,128]{4,2,3,1,0:T(8,128)(2,1)}), bf16[64,2,128,2,128]{4,2,3,1,0:T(8,128)(2,1)}, u32[]{:S(2)}, u32[]{:S(2)}) %all-to-all-start.2) | async-done | bytes 8388640 | tf_op jit(solution)/shard_map/all_to_all | solution.py:63
  325.7 6.9 %all-to-all-start.3 = ((bf16[16,8,128]{2,0,1:T(8,128)(2,1)}), bf16[16,8,128]{2,0,1:T(8,128)(2,1)S(1)}, u32[]{:S(2)}, u32[]{:S(2)}) async-start(bf16[16,8,128]{2,0,1:T(8,128)(2,1)} %copy_bitcast_fusion.1), calls=%async_computation.3 | async-start | bytes 65536 | tf_op jit(solution)/shard_map/all_to_all | solution.py:39
  332.6 6.4 %gather_fusion.1 = bf16[64,128,2,128]{3,1,2,0:T(8,128)(2,1)} fusion(bf16[128,128,2,128]{3,1,2,0:T(8,128)(2,1)} %bitcast.34, s32[1024]{0:T(1024)S(1)} %pad_clamp_fusion), kind=kCustom, calls=%fused_computation.1 | custom fusion | bytes 8388864 | tf_op jit(solution)/shard_map/gather | solution.py:64
  339.1 4.7 %fusion.39 = (bf16[64,128,1,128]{3,1,2,0:T(8,128)(2,1)}, bf16[64,128,1,128]{3,1,2,0:T(8,128)(2,1)}) fusion(bf16[64,128,2,128]{3,1,2,0:T(8,128)(2,1)} %gather_fusion.1), kind=kLoop, calls=%fused_computation.63 | loop fusion | bytes 8388608 | tf_op jit(solution)/shard_map/slice | solution.py:66
  343.8 13.9 %while.22 = (s32[]{:T(128)}, f32[1,8,128]{2,1,0:T(8,128)S(1)}, pred[8,1024]{1,0:T(8,128)(4,1)S(1)}, bf16[8,1024,1,128]{3,1,2,0:T(8,128)(2,1)}, bf16[128,1,8,128]{3,0,2,1:T(8,128)(2,1)S(1)}, /*index=5*/s32[]{:T(128)}) while((s32[]{:T(128)}, f32[1,8,128]{2,1,0:T(8,128)S(1)}, pred[8,1024]{1,0:T(8,128)(4,1)S(1)}, ...), condition=%wide.region_6.7_spmd, body=%wide.region_4.6_spmd.sunk | while | flops 271581184 | bytes 544329 | solution.py:91
  343.8 1.7 fusion.54
  345.6 1.7 fusion.54
  347.3 1.7 fusion.54
  349.1 1.7 fusion.54
  350.8 1.7 fusion.54
  352.6 1.7 fusion.54
  354.3 1.7 fusion.54
  356.0 1.7 fusion.54
  357.8 0.1 fusion.31
  357.8 0.0 all-to-all-done.3
  357.9 0.3 convolution_bitcast_fusion
  358.1 0.2 copy.82
  358.3 34.3 %while.23 = (s32[]{:T(128)}, f32[1,8,128]{2,1,0:T(8,128)S(1)}, f32[128,1,8,128]{0,3,2,1:T(8,128)S(1)}, pred[8,1024]{1,0:T(8,128)(4,1)S(1)}, bf16[8,1024,1,128]{3...) while((s32[]{:T(128)}, f32[1,8,128]{2,1,0:T(8,128)S(1)}, ...), condition=%wide.region_10.11_spmd, body=%wide.region_8.10_spmd.sunk | while | flops 545390592 | bytes 10253409 | solution.py:111
  358.4 2.0 fusion.57
  360.4 2.2 fusion.58
  362.7 2.1 fusion.57
  364.7 2.2 fusion.58
  367.0 2.1 fusion.57
  369.0 2.2 fusion.58
  371.3 2.1 fusion.57
  373.3 2.2 fusion.58
  375.6 2.1 fusion.57
  377.6 2.2 fusion.58
  379.8 2.1 fusion.57
  381.9 2.2 fusion.58
  384.1 2.1 fusion.57
  386.2 2.2 fusion.58
  388.4 2.1 fusion.57
  390.5 2.2 fusion.58
  392.7 0.1 divide_convert_fusion
  392.8 0.5 broadcast.142
  393.3 0.8 reduce.10
  394.1 0.1 copy.107
  394.2 0.2 reshape.256
  394.4 18.7 %all_to_all.65 = bf16[8,2,8192]{2,1,0:T(2,128)(2,1)S(1)} all-to-all(bf16[8,2,8192]{2,1,0:T(2,128)(2,1)S(1)} %reshape.256), channel_id=1, replica_groups=mesh['dp'=64,'tensor'=8] {'tensor'}, dimensions={0} | all-to-all | bytes 524288 | tf_op jit(solution)/shard_map/all_to_all | solution.py:116
  413.1 0.3 reshape.257
  413.4 0.1 copy.91
  413.5 0.7 copy.97
  (46 shorter events, 0.7 us)
Async XLA Ops:
  0.0 104.1 %copy-start = (bf16[32,128,2,128]{3,2,1,0:T(2,128)(2,1)S(1)}, bf16[32,128,2,128]{3,2,1,0:T(2,128)(2,1)}, u32[]{:S(2)}) copy-start(bf16[32,128,2,128]{3,2,1,0:T(2,128)(2,1)} %param.14) | copy-start | bytes 6291460
  1.5 55.1 %all-to-all-start = ((bf16[16,8,128]{2,0,1:T(8,128)(2,1)}), bf16[16,8,128]{2,0,1:T(8,128)(2,1)S(1)}, u32[]{:S(2)}, u32[]{:S(2)}) async-start(bf16[16,8,128]{2,0,1:T(8,128)(2,1)} %copy_bitcast_fusion.2), calls=%async_computation | async-start | bytes 65536 | tf_op jit(solution)/shard_map/all_to_all | solution.py:38
  56.6 76.1 %all-to-all-start.1 = ((bf16[16,8,1024]{2,0,1:T(8,128)(2,1)}), bf16[16,8,1024]{2,0,1:T(8,128)(2,1)S(1)}, u32[]{:S(2)}, u32[]{:S(2)}) async-start(bf16[16,8,1024]{2,0,1:T(8,128)(2,1)} %bitcast.179), calls=%async_computation.1 | async-start | bytes 524288 | tf_op jit(solution)/shard_map/all_to_all | solution.py:37
  132.8 7.8 %copy-start.2 = (s32[1,64,1]{1,2,0:T(1,128)S(1)}, s32[1,64,1]{1,2,0:T(1,128)}, u32[]{:S(2)}) copy-start(s32[1,64,1]{1,2,0:T(1,128)} %param.15) | copy-start | bytes 772
  132.8 8.1 %copy-start.1 = (bf16[16,1024]{1,0:T(8,128)(2,1)S(1)}, bf16[16,1024]{1,0:T(8,128)(2,1)}, u32[]{:S(2)}) copy-start(bf16[16,1024]{1,0:T(8,128)(2,1)} %param.13) | copy-start | bytes 98308
  132.8 192.9 %all-to-all-start.2 = ((bf16[64,2,128,2,128]{4,2,3,1,0:T(8,128)(2,1)}), bf16[64,2,128,2,128]{4,2,3,1,0:T(8,128)(2,1)}, u32[]{:S(2)}, u32[]{:S(2)}) async-start(bf16[64,2,128,2,128]{4,2,3,1,0:T(8,128)(2,1)} %copy.77), calls=%async_computation.2 | async-start | bytes 16777216 | tf_op jit(solution)/shard_map/all_to_all | solution.py:63
  325.7 32.1 %all-to-all-start.3 = ((bf16[16,8,128]{2,0,1:T(8,128)(2,1)}), bf16[16,8,128]{2,0,1:T(8,128)(2,1)S(1)}, u32[]{:S(2)}, u32[]{:S(2)}) async-start(bf16[16,8,128]{2,0,1:T(8,128)(2,1)} %copy_bitcast_fusion.1), calls=%async_computation.3 | async-start | bytes 65536 | tf_op jit(solution)/shard_map/all_to_all | solution.py:39
where the time goes:
time: 416 us; the launch traced here: 414 us
  waiting for transfers between devices  184 us (44%)
  blocking collectives  103 us (25%)
  matrix products  47.7 us (11%)
  local copies, waits for them, and re-layouts  46.6 us (11%)
  starting transfers between devices  28.7 us (7%)
    all_to_all x1, waiting for transfers between devices, local(): lax.all_to_all(picked, 'dp', split_axis=0, concat_axis=0, tiled=True)  184 us
    all_gather x1, blocking collectives, local(): lax.all_gather(sources, 'dp', axis=0, tiled=True)  45.8 us
    all_gather x1, blocking collectives, local(): lax.all_gather(block_ids, 'dp', axis=0, tiled=True)  38.3 us
    dot_general x16, matrix products, score_block(): jnp.einsum('nhgd,khd->hgnk', query_rows, keys, preferred_element_type=jnp...  29.8 us
    gather x1, local copies, waits for them, and re-layouts, local(): picked = hist_kv[send_table.reshape(-1)]  19.5 us
    all_to_all x1, blocking collectives, local(): lax.all_to_all(result, 'tensor', split_axis=0, concat_axis=1, tiled=True)  18.7 us
    dot_general x8, matrix products, sum_step(): jnp.einsum('hgnk,khd->nhgd', weights.astype(jnp.bfloat16), vals, preferre...  17.4 us
    reshape x1, local copies, waits for them, and re-layouts, local(): picked = picked.reshape(groups, capacity, block_len, 2, width)  9.15 us
  transfers between devices with their start and end apart: 4, of which 1 were waited for; matrix products, arithmetic and copies ran while one was open for 14% of the time, Pallas kernels for 0%

commit v1 on v0

--- a/solution.py
+++ b/solution.py
@@ -7,6 +7,12 @@
 HQ = 64
 KVH = 8
 HD = 128
+
+
+def chains_return_all(obj, across, join_dim):
+    w2 = jnp.stack([obj for _ in range(jax.lax.axis_size(across))])
+    upper = jax.lax.all_to_all(w2, across, 0, 0)
+    return jnp.concatenate(upper, axis=join_dim)
 
 
 def slot_ranks(src_rows):
@@ -48,7 +54,7 @@
     ranks = slot_ranks(src_list)
     all_src, all_ids = (
         lax.all_gather(sources, "dp", axis=0, tiled=True),
-        lax.all_gather(block_ids, "dp", axis=0, tiled=True),
+        chains_return_all(block_ids, "dp", join_dim=0),
     )
     all_src = all_src.reshape(groups, slots)
     owners = jnp.reshape(lax.axis_index("dp"), (1,))

time: 416 us -> 393 us (0.945)
  blocking collectives: 103 us -> 60.2 us
  starting transfers between devices: 28.7 us -> 40.4 us
  waiting for transfers between devices: 184 us -> 191 us
    all_gather x1 -> x0, blocking collectives: 38.3 us -> none  [local(): lax.all_gather(block_ids, 'dp', axis=0, tiled=True)]
    all_to_all x0 -> x1, starting transfers between devices: none -> 14.8 us  [chains_return_all(): upper = jax.lax.all_to_all(w2, across, 0, 0)]
    all_to_all x1, waiting for transfers between devices: 0.01 us -> 6.86 us  [local(): lax.all_to_all(k_parts, 'tensor', split_axis=1, concat_axis=0, tiled=True)]
    all_gather x1, blocking collectives: 45.8 us -> 41.4 us  [local(): lax.all_gather(sources, 'dp', axis=0, tiled=True)]
  transfers between devices with their start and end apart: 4 -> 5, of which waited for: 1 -> 2; matrix products, arithmetic and copies ran while one was open for 14% -> 15% of each run, Pallas kernels for 0% -> 0%
where the time goes in v1:
time: 393 us; the launch traced here: 392 us
  waiting for transfers between devices  191 us (49%)
  blocking collectives  60.2 us (15%)
  local copies, waits for them, and re-layouts  47.8 us (12%)
  matrix products  47.7 us (12%)
  starting transfers between devices  40.4 us (10%)
    all_to_all x1, waiting for transfers between devices, local(): lax.all_to_all(picked, 'dp', split_axis=0, concat_axis=0, tiled=True)  184 us
    all_gather x1, blocking collectives, local(): lax.all_gather(sources, 'dp', axis=0, tiled=True)  41.4 us
    dot_general x16, matrix products, score_block(): jnp.einsum('nhgd,khd->hgnk', query_rows, keys, preferred_element_type=jnp...  29.9 us
    gather x1, local copies, waits for them, and re-layouts, local(): picked = hist_kv[send_table.reshape(-1)]  19.5 us
    all_to_all x1, blocking collectives, local(): lax.all_to_all(result, 'tensor', split_axis=0, concat_axis=1, tiled=True)  18.8 us
    dot_general x8, matrix products, sum_step(): jnp.einsum('hgnk,khd->nhgd', weights.astype(jnp.bfloat16), vals, preferre...  17.4 us
    all_to_all x1, starting transfers between devices, chains_return_all(): upper = jax.lax.all_to_all(w2, across, 0, 0)  14.8 us
    reshape x1, local copies, waits for them, and re-layouts, local(): picked = picked.reshape(groups, capacity, block_len, 2, width)  9.15 us
  transfers between devices with their start and end apart: 5, of which 2 were waited for; matrix products, arithmetic and copies ran while one was open for 15% of the time, Pallas kernels for 0%

profile of v1, /device:TPU:1, one launch (start us, length us, event | category | flops | bytes accessed | tf_op | source)
XLA Modules:
  0.0 391.5 jit_solution(3708033605290939067)
XLA Ops:
  0.0 1.4 stack.2
  1.4 14.8 %all-to-all-start.2 = ((s32[64,1,64]{2,1,0:T(1,128)}), s32[64,1,64]{2,1,0:T(1,128)S(1)}, u32[]{:S(2)}, u32[]{:S(2)}) async-start(s32[64,1,64]{2,1,0:T(1,128)} %stack.2), calls=%async_computation.2 | async-start | bytes 65536 | tf_op jit(solution)/shard_map/all_to_all | solution.py:14
  16.3 41.4 %all_gather.3 = s32[64,64,1]{1,2,0:T(1,128)S(1)} all-gather(s32[1,64,1]{1,2,0:T(1,128)} %param.15), channel_id=1, replica_groups=mesh['dp'=64,'tensor'=8] {'dp'}, dimensions={0}, use_global_device_ids=true | all-gather | bytes 16640 | tf_op jit(solution)/shard_map/all_gather | solution.py:56
  57.7 1.4 copy_bitcast_fusion.2
  59.1 1.7 copy.106
  60.7 0.0 all-to-all-done.2
  60.7 6.8 %all-to-all-start = ((bf16[16,8,128]{2,0,1:T(8,128)(2,1)}), bf16[16,8,128]{2,0,1:T(8,128)(2,1)S(1)}, u32[]{:S(2)}, u32[]{:S(2)}) async-start(bf16[16,8,128]{2,0,1:T(8,128)(2,1)} %copy_bitcast_fusion.2), calls=%async_computation | async-start | bytes 65536 | tf_op jit(solution)/shard_map/all_to_all | solution.py:44
  67.6 6.9 %all-to-all-done = bf16[16,8,128]{2,0,1:T(8,128)(2,1)S(1)} async-done(((bf16[16,8,128]{2,0,1:T(8,128)(2,1)}), bf16[16,8,128]{2,0,1:T(8,128)(2,1)S(1)}, u32[]{:S(2)}, u32[]{:S(2)}) %all-to-all-start) | async-done | bytes 32800 | tf_op jit(solution)/shard_map/all_to_all | solution.py:44
  74.4 3.4 all-to-all-start.1
  77.9 1.9 convert_reduce_fusion
  79.7 0.1 select_reduce_fusion
  79.8 0.1 copy.76
  79.9 0.1 reshape_reshape.3
  80.1 19.5 %gather_fusion = bf16[128,128,2,128]{3,2,1,0:T(2,128)(2,1)} fusion(bf16[32,128,2,128]{3,2,1,0:T(2,128)(2,1)S(1)} %copy-done, s32[1024]{0:T(1024)S(1)} %pad_clamp_fusion.1), kind=kCustom, calls=%fused_computation | custom fusion | bytes 16777728 | tf_op jit(solution)/shard_map/gather | solution.py:64
  99.6 9.1 %copy.77 = bf16[64,2,128,2,128]{4,2,3,1,0:T(8,128)(2,1)} copy(bf16[64,2,128,2,128]{4,3,2,1,0:T(2,128)(2,1)} %bitcast.211) | data formatting | bytes 16777216 | tf_op jit(solution)/shard_map/reshape | solution.py:67
  108.7 0.0 all-to-all-done.1
  108.7 8.5 %all-to-all-start.3 = ((bf16[64,2,128,2,128]{4,2,3,1,0:T(8,128)(2,1)}), bf16[64,2,128,2,128]{4,2,3,1,0:T(8,128)(2,1)}, u32[]{:S(2)}, u32[]{:S(2)}) async-start(bf16[64,2,128,2,128]{4,2,3,1,0:T(8,128)(2,1)} %copy.77), calls=%async_computation.3 | async-start | bytes 16777216 | tf_op jit(solution)/shard_map/all_to_all | solution.py:69
  117.9 0.2 convert_reduce_fusion.1
  118.2 0.1 broadcast_bitcast_fusion
  118.2 0.6 copy_bitcast_fusion.1
  119.0 0.2 fusion.40
  119.2 183.8 %all-to-all-done.3 = bf16[64,2,128,2,128]{4,2,3,1,0:T(8,128)(2,1)} async-done(((bf16[64,2,128,2,128]{4,2,3,1,0:T(8,128)(2,1)}), bf16[64,2,128,2,128]{4,2,3,1,0:T(8,128)(2,1)}, u32[]{:S(2)}, u32[]{:S(2)}) %all-to-all-start.3) | async-done | bytes 8388640 | tf_op jit(solution)/shard_map/all_to_all | solution.py:69
  303.0 6.8 %all-to-all-start.4 = ((bf16[16,8,128]{2,0,1:T(8,128)(2,1)}), bf16[16,8,128]{2,0,1:T(8,128)(2,1)S(1)}, u32[]{:S(2)}, u32[]{:S(2)}) async-start(bf16[16,8,128]{2,0,1:T(8,128)(2,1)} %copy_bitcast_fusion.1), calls=%async_computation.4 | async-start | bytes 65536 | tf_op jit(solution)/shard_map/all_to_all | solution.py:45
  309.9 6.4 %gather_fusion.1 = bf16[64,128,2,128]{3,1,2,0:T(8,128)(2,1)} fusion(bf16[128,128,2,128]{3,1,2,0:T(8,128)(2,1)} %bitcast.34, s32[1024]{0:T(1024)S(1)} %pad_clamp_fusion), kind=kCustom, calls=%fused_computation.1 | custom fusion | bytes 8388864 | tf_op jit(solution)/shard_map/gather | solution.py:70
  316.3 4.7 %fusion.39 = (bf16[64,128,1,128]{3,1,2,0:T(8,128)(2,1)}, bf16[64,128,1,128]{3,1,2,0:T(8,128)(2,1)}) fusion(bf16[64,128,2,128]{3,1,2,0:T(8,128)(2,1)} %gather_fusion.1), kind=kLoop, calls=%fused_computation.63 | loop fusion | bytes 8388608 | tf_op jit(solution)/shard_map/slice | solution.py:72
  321.0 13.9 %while.22 = (s32[]{:T(128)}, f32[1,8,128]{2,1,0:T(8,128)S(1)}, pred[8,1024]{1,0:T(8,128)(4,1)S(1)}, bf16[8,1024,1,128]{3,1,2,0:T(8,128)(2,1)}, bf16[128,1,8,128]{3,0,2,1:T(8,128)(2,1)S(1)}, /*index=5*/s32[]{:T(128)}) while((s32[]{:T(128)}, f32[1,8,128]{2,1,0:T(8,128)S(1)}, pred[8,1024]{1,0:T(8,128)(4,1)S(1)}, ...), condition=%wide.region_6.7_spmd, body=%wide.region_4.6_spmd.sunk | while | flops 271581184 | bytes 544329 | solution.py:97
  321.1 1.7 fusion.54
  322.8 1.7 fusion.54
  324.6 1.7 fusion.54
  326.3 1.7 fusion.54
  328.0 1.7 fusion.54
  329.8 1.7 fusion.54
  331.5 1.7 fusion.54
  333.3 1.7 fusion.54
  335.0 0.1 fusion.31
  335.1 0.0 all-to-all-done.4
  335.1 0.3 convolution_bitcast_fusion
  335.4 0.2 copy.82
  335.6 34.4 %while.23 = (s32[]{:T(128)}, f32[1,8,128]{2,1,0:T(8,128)S(1)}, f32[128,1,8,128]{0,3,2,1:T(8,128)S(1)}, pred[8,1024]{1,0:T(8,128)(4,1)S(1)}, bf16[8,1024,1,128]{3...) while((s32[]{:T(128)}, f32[1,8,128]{2,1,0:T(8,128)S(1)}, ...), condition=%wide.region_10.11_spmd, body=%wide.region_8.10_spmd.sunk | while | flops 545390592 | bytes 10253409 | solution.py:117
  335.6 2.1 fusion.57
  337.7 2.2 fusion.58
  339.9 2.1 fusion.57
  342.0 2.2 fusion.58
  344.2 2.1 fusion.57
  346.3 2.2 fusion.58
  348.5 2.1 fusion.57
  350.5 2.2 fusion.58
  352.8 2.1 fusion.57
  354.8 2.2 fusion.58
  357.1 2.1 fusion.57
  359.1 2.2 fusion.58
  361.4 2.1 fusion.57
  363.4 2.2 fusion.58
  365.7 2.1 fusion.57
  367.7 2.2 fusion.58
  369.9 0.1 divide_convert_fusion
  370.0 0.5 broadcast.144
  370.5 0.8 reduce.10
  371.3 0.1 copy.107
  371.5 0.2 reshape.257
  371.7 18.8 %all_to_all.70 = bf16[8,2,8192]{2,1,0:T(2,128)(2,1)S(1)} all-to-all(bf16[8,2,8192]{2,1,0:T(2,128)(2,1)S(1)} %reshape.257), channel_id=1, replica_groups=mesh['dp'=64,'tensor'=8] {'tensor'}, dimensions={0} | all-to-all | bytes 524288 | tf_op jit(solution)/shard_map/all_to_all | solution.py:122
  390.4 0.3 reshape.258
  390.7 0.1 copy.91
  390.8 0.7 copy.97
  (48 shorter events, 0.7 us)
Async XLA Ops:
  0.0 80.1 %copy-start = (bf16[32,128,2,128]{3,2,1,0:T(2,128)(2,1)S(1)}, bf16[32,128,2,128]{3,2,1,0:T(2,128)(2,1)}, u32[]{:S(2)}) copy-start(bf16[32,128,2,128]{3,2,1,0:T(2,128)(2,1)} %param.14) | copy-start | bytes 6291460
  1.4 59.3 %all-to-all-start.2 = ((s32[64,1,64]{2,1,0:T(1,128)}), s32[64,1,64]{2,1,0:T(1,128)S(1)}, u32[]{:S(2)}, u32[]{:S(2)}) async-start(s32[64,1,64]{2,1,0:T(1,128)} %stack.2), calls=%async_computation.2 | async-start | bytes 65536 | tf_op jit(solution)/shard_map/all_to_all | solution.py:14
  60.7 13.7 %all-to-all-start = ((bf16[16,8,128]{2,0,1:T(8,128)(2,1)}), bf16[16,8,128]{2,0,1:T(8,128)(2,1)S(1)}, u32[]{:S(2)}, u32[]{:S(2)}) async-start(bf16[16,8,128]{2,0,1:T(8,128)(2,1)} %copy_bitcast_fusion.2), calls=%async_computation | async-start | bytes 65536 | tf_op jit(solution)/shard_map/all_to_all | solution.py:44
  74.4 34.3 %all-to-all-start.1 = ((bf16[16,8,1024]{2,0,1:T(8,128)(2,1)}), bf16[16,8,1024]{2,0,1:T(8,128)(2,1)S(1)}, u32[]{:S(2)}, u32[]{:S(2)}) async-start(bf16[16,8,1024]{2,0,1:T(8,128)(2,1)} %bitcast.179), calls=%async_computation.1 | async-start | bytes 524288 | tf_op jit(solution)/shard_map/all_to_all | solution.py:43
  108.7 9.2 %copy-start.2 = (s32[1,64,1]{1,2,0:T(1,128)S(1)}, s32[1,64,1]{1,2,0:T(1,128)}, u32[]{:S(2)}) copy-start(s32[1,64,1]{1,2,0:T(1,128)} %param.15) | copy-start | bytes 772
  108.7 9.5 %copy-start.1 = (bf16[16,1024]{1,0:T(8,128)(2,1)S(1)}, bf16[16,1024]{1,0:T(8,128)(2,1)}, u32[]{:S(2)}) copy-start(bf16[16,1024]{1,0:T(8,128)(2,1)} %param.13) | copy-start | bytes 98308
  108.7 194.3 %all-to-all-start.3 = ((bf16[64,2,128,2,128]{4,2,3,1,0:T(8,128)(2,1)}), bf16[64,2,128,2,128]{4,2,3,1,0:T(8,128)(2,1)}, u32[]{:S(2)}, u32[]{:S(2)}) async-start(bf16[64,2,128,2,128]{4,2,3,1,0:T(8,128)(2,1)} %copy.77), calls=%async_computation.3 | async-start | bytes 16777216 | tf_op jit(solution)/shard_map/all_to_all | solution.py:69
  303.0 32.1 %all-to-all-start.4 = ((bf16[16,8,128]{2,0,1:T(8,128)(2,1)}), bf16[16,8,128]{2,0,1:T(8,128)(2,1)S(1)}, u32[]{:S(2)}, u32[]{:S(2)}) async-start(bf16[16,8,128]{2,0,1:T(8,128)(2,1)} %copy_bitcast_fusion.1), calls=%async_computation.4 | async-start | bytes 65536 | tf_op jit(solution)/shard_map/all_to_all | solution.py:45
